TPU v7x, 128 devices: a whole 4x4x4 slice. The times are simulated.
128 devices in a mesh: row: 8 (over z, x_hi), col: 16 (over x_lo, y, core).
Axes of the slice: x: 4 (x_hi: 2, x_lo: 2; x = x_hi * 2 + x_lo), y: 4, z: 4, core: 2. Of those that a mesh axis runs over, the one named last changes fastest.
Arguments:
- embeddings: bfloat16 [32768, 768], P(('row', 'col'))
- spread: bfloat16 [32768], P(('row', 'col')), may hold values from 1 to 16
- features: bfloat16 [32768, 256], P(('row', 'col')), may hold values from -160 to 160
- block_list: int32 [256], replicated, may hold values from 0 to 63
- list_pairs: int32 [64, 64], replicated, may hold values from 0 to 1, as said below
Outputs:
- smoothed: float32 [32768, 256], P(('row', 'col'))
Inputs may be any that keep to these rules, and one draw needn't show every extreme that they name: `list_pairs`: symmetric, with ones on the diagonal.
All inputs are finite; a program needn't handle non-finite values.
Results may differ from a plain program's by a relative error of at most 0.0029.
Values may be sent and summed in bfloat16 or wider, within the bound.
A program may use at most 64 MiB of HBM per device.

v0:
```python
import math
import jax
import jax.numpy as jnp
from jax import lax
from jax.sharding import PartitionSpec as P

BLK = 128
LISTS = 64


def active_table(block_list, list_pairs, row_blocks, col_blocks):
    count = block_list.shape[0]
    lists_onehot = (block_list[:, None] == jnp.arange(LISTS, dtype=jnp.int32)[None, :]).astype(
        jnp.float32
    )
    pair_table = list_pairs.astype(jnp.float32)
    row_select = (row_blocks[:, None] == jnp.arange(count, dtype=jnp.int32)[None, :]).astype(
        jnp.float32
    )
    col_select = (col_blocks[:, None] == jnp.arange(count, dtype=jnp.int32)[None, :]).astype(
        jnp.float32
    )
    row_onehot = jnp.dot(row_select, lists_onehot, precision=lax.Precision.HIGHEST)
    col_onehot = jnp.dot(col_select, lists_onehot, precision=lax.Precision.HIGHEST)
    joined = jnp.dot(row_onehot, pair_table, precision=lax.Precision.HIGHEST)
    return jnp.dot(joined, col_onehot.T, precision=lax.Precision.HIGHEST)


def shards(embeddings, spread, features, block_list, list_pairs):
    rows_x, rows_beta = (
        lax.all_gather(embeddings, "col", axis=0, tiled=True),
        lax.all_gather(spread, "col", axis=0, tiled=True),
    )
    cols_x, cols_beta, cols_feat = (
        lax.all_gather(embeddings, "row", axis=0, tiled=True),
        lax.all_gather(spread, "row", axis=0, tiled=True),
        lax.all_gather(features, "row", axis=0, tiled=True),
    )
    own_count = embeddings.shape[0]
    col_size = lax.axis_size("col")
    row_index = lax.axis_index("row")
    col_index = lax.axis_index("col")
    total_rows = rows_x.shape[0]
    total_cols = cols_x.shape[0]
    row_ids = row_index * total_rows + jnp.arange(total_rows, dtype=jnp.int32)
    local_index = jnp.arange(total_cols, dtype=jnp.int32)
    col_ids = (
        local_index // own_count * col_size + col_index
    ) * own_count + local_index % own_count
    active = active_table(block_list, list_pairs, row_ids[::BLK] // BLK, col_ids[::BLK] // BLK)
    col_blocks = active.shape[1]
    row_norm = jnp.sum(jnp.square(rows_x.astype(jnp.float32)), axis=1)
    col_norm = jnp.sum(jnp.square(cols_x.astype(jnp.float32)), axis=1)
    row_bw = rows_beta.astype(jnp.float32)
    col_bw = cols_beta.astype(jnp.float32)

    def block_terms(start, size):
        row_emb = lax.dynamic_slice_in_dim(rows_x, start, size, 0)
        norm_part = lax.dynamic_slice_in_dim(row_norm, start, size, 0)
        beta_part = lax.dynamic_slice_in_dim(row_bw, start, size, 0)
        ids_part = lax.dynamic_slice_in_dim(row_ids, start, size, 0)
        inner = lax.dot_general(
            row_emb, cols_x, (((1,), (1,)), ((), ())), preferred_element_type=jnp.float32
        )
        dist = norm_part[:, None] + col_norm[None, :] - 2.0 * inner
        active_part = lax.dynamic_slice_in_dim(active, start // BLK, size // BLK, 0)
        expanded = jnp.broadcast_to(
            active_part[:, None, :, None], (size // BLK, BLK, col_blocks, BLK)
        )
        mask = expanded.reshape(size, total_cols) * (ids_part[:, None] != col_ids[None, :]).astype(
            jnp.float32
        )
        near = mask * jnp.exp(-beta_part[:, None] * dist)
        return (mask, dist, near)

    block_rows = math.gcd(total_rows, 512)
    starts = jnp.arange(total_rows // block_rows, dtype=jnp.int32) * block_rows
    row_partial = lax.map(
        lambda start: jnp.sum(block_terms(start, block_rows)[2], axis=1), starts
    ).reshape(total_rows)
    row_totals = lax.psum(row_partial, "col")
    own_totals = lax.dynamic_slice_in_dim(row_totals, col_index * own_count, own_count, 0)
    col_totals = lax.all_gather(own_totals, "row", axis=0, tiled=True)
    size = math.gcd(total_rows, 512)

    def one_block(begin):
        mask, dist, near = block_terms(begin, size)
        far = mask * jnp.exp(-col_bw[None, :] * dist)
        total_part = lax.dynamic_slice_in_dim(row_totals, begin, size, 0)
        weight = ((near / total_part[:, None] + far / col_totals[None, :]) * 0.5).astype(
            jnp.bfloat16
        )
        return jnp.dot(weight, cols_feat, preferred_element_type=jnp.float32)

    begins = 0 + jnp.arange(total_rows // size, dtype=jnp.int32) * size
    partial_out = lax.map(one_block, begins).reshape(total_rows, cols_feat.shape[1])
    summed = lax.psum(partial_out, "col")
    return lax.dynamic_slice_in_dim(summed, col_index * own_count, own_count, 0)


def solution(mesh):
    return jax.shard_map(
        shards,
        mesh=mesh,
        in_specs=(P(("row", "col"), None), P(("row", "col")), P(("row", "col"), None), P(), P()),
        out_specs=P(("row", "col"), None),
        check_vma=False,
    )
```

profile of v0, /device:TPU:1, one launch (start us, length us, event | category | flops | bytes accessed | tf_op | source)
XLA Modules:
  0.0 548.1 jit_solution(9659464464459559050)
XLA Ops:
  9.5 21.2 %all-gather = bf16[16,1,256]{2,1,0:T(2,128)(2,1)S(1)} all-gather(bf16[1,1,256]{2,1,0:T(2,128)(2,1)S(1)} %reshape.44), channel_id=1, replica_groups=mesh['row'=8,'col'=16] {'col'}, dimensions={0}, use_global_device_ids=true | all-gather | bytes 8704 | tf_op jit(solution)/shard_map/all_gather | solution.py:32
  30.6 20.6 %all-gather.1 = bf16[8,1,256]{2,1,0:T(2,128)(2,1)S(1)} all-gather(bf16[1,1,256]{2,1,0:T(2,128)(2,1)S(1)} %reshape.44), channel_id=1, replica_groups=mesh['row'=8,'col'=16] {'row'}, dimensions={0}, use_global_device_ids=true | all-gather | bytes 4608 | tf_op jit(solution)/shard_map/all_gather | solution.py:36
  54.4 21.0 %all-gather.9.cloned.1.call-done = bf16[2048,768]{1,0:T(8,128)(2,1)} async-done(((bf16[256,768]{1,0:T(8,128)(2,1)}), bf16[2048,768]{1,0:T(8,128)(2,1)}) %all-gather.9.cloned.1.call-update) | async-done | bytes 3145744 | tf_op jit(solution)/shard_map/all_gather | solution.py:35
  75.3 2.7 multiply_reduce_fusion.1
  78.1 39.8 %all-gather.7.cloned.1.call-done = bf16[4096,768]{1,0:T(8,128)(2,1)} async-done(((bf16[256,768]{1,0:T(8,128)(2,1)}), bf16[4096,768]{1,0:T(8,128)(2,1)}) %all-gather.7.cloned.1.call-update) | async-done | bytes 6291472 | tf_op jit(solution)/shard_map/all_gather | solution.py:31
  117.9 4.1 multiply_reduce_fusion
  122.0 102.0 %while.26 = (s32[]{:T(128)}, f32[8,512]{1,0:T(8,128)S(1)}, s32[8]{0:T(128)S(1)}, s32[4096]{0:T(1024)S(1)}, f32[32,16]{1,0:T(8,128)S(1)}, /*index=5*/f32[4096]{0:...) while((s32[]{:T(128)}, f32[8,512]{1,0:T(8,128)S(1)}, ...), condition=%wide.region_4.5_spmd.clone, body=%wide.region_2.4_spmd.clone.sunk | while | flops 1619034112 | bytes 12371102 | solution.py:78
  125.1 2.4 broadcast_in_dim.65
  129.0 5.8 %fusion.78 = f32[512]{0:T(512)S(1)} fusion(f32[64,8,16,128]{3,2,1,0:T(8,128)} %bitcast.66, bf16[2048,768]{1,0:T(8,128)(2,1)S(1)} %get-tuple-element.698, f32[2048]{0:T(1024)S(1)} %get-tuple-element.696, f32[512]{0:T(512)S(1)} %dynamic_slice.127, f32[512]{0:T(512)S(1)} %dynamic-slice_negate_fusion.4, s32[2048]{0:T(1024)S(1)} %fusion.77, ...), kind=kOutput, calls=%fused_computation.4.clone.1 | convolution fusion | flops 1619000832 | bytes 8151044 | tf_op jit(solution)/shard_map/while/body/eval_jaxpr/dot_general | solution.py:62
  137.9 2.4 broadcast_in_dim.65
  141.8 5.7 %fusion.78 = f32[512]{0:T(512)S(1)} fusion(f32[64,8,16,128]{3,2,1,0:T(8,128)} %bitcast.66, bf16[2048,768]{1,0:T(8,128)(2,1)S(1)} %get-tuple-element.698, f32[2048]{0:T(1024)S(1)} %get-tuple-element.696, f32[512]{0:T(512)S(1)} %dynamic_slice.127, f32[512]{0:T(512)S(1)} %dynamic-slice_negate_fusion.4, s32[2048]{0:T(1024)S(1)} %fusion.77, ...), kind=kOutput, calls=%fused_computation.4.clone.1 | convolution fusion | flops 1619000832 | bytes 8151044 | tf_op jit(solution)/shard_map/while/body/eval_jaxpr/dot_general | solution.py:62
  150.7 2.4 broadcast_in_dim.65
  154.6 5.7 %fusion.78 = f32[512]{0:T(512)S(1)} fusion(f32[64,8,16,128]{3,2,1,0:T(8,128)} %bitcast.66, bf16[2048,768]{1,0:T(8,128)(2,1)S(1)} %get-tuple-element.698, f32[2048]{0:T(1024)S(1)} %get-tuple-element.696, f32[512]{0:T(512)S(1)} %dynamic_slice.127, f32[512]{0:T(512)S(1)} %dynamic-slice_negate_fusion.4, s32[2048]{0:T(1024)S(1)} %fusion.77, ...), kind=kOutput, calls=%fused_computation.4.clone.1 | convolution fusion | flops 1619000832 | bytes 8151044 | tf_op jit(solution)/shard_map/while/body/eval_jaxpr/dot_general | solution.py:62
  163.4 2.4 broadcast_in_dim.65
  167.3 5.7 %fusion.78 = f32[512]{0:T(512)S(1)} fusion(f32[64,8,16,128]{3,2,1,0:T(8,128)} %bitcast.66, bf16[2048,768]{1,0:T(8,128)(2,1)S(1)} %get-tuple-element.698, f32[2048]{0:T(1024)S(1)} %get-tuple-element.696, f32[512]{0:T(512)S(1)} %dynamic_slice.127, f32[512]{0:T(512)S(1)} %dynamic-slice_negate_fusion.4, s32[2048]{0:T(1024)S(1)} %fusion.77, ...), kind=kOutput, calls=%fused_computation.4.clone.1 | convolution fusion | flops 1619000832 | bytes 8151044 | tf_op jit(solution)/shard_map/while/body/eval_jaxpr/dot_general | solution.py:62
  176.2 2.4 broadcast_in_dim.65
  180.1 5.7 %fusion.78 = f32[512]{0:T(512)S(1)} fusion(f32[64,8,16,128]{3,2,1,0:T(8,128)} %bitcast.66, bf16[2048,768]{1,0:T(8,128)(2,1)S(1)} %get-tuple-element.698, f32[2048]{0:T(1024)S(1)} %get-tuple-element.696, f32[512]{0:T(512)S(1)} %dynamic_slice.127, f32[512]{0:T(512)S(1)} %dynamic-slice_negate_fusion.4, s32[2048]{0:T(1024)S(1)} %fusion.77, ...), kind=kOutput, calls=%fused_computation.4.clone.1 | convolution fusion | flops 1619000832 | bytes 8151044 | tf_op jit(solution)/shard_map/while/body/eval_jaxpr/dot_general | solution.py:62
  192.8 5.7 %fusion.78 = f32[512]{0:T(512)S(1)} fusion(f32[64,8,16,128]{3,2,1,0:T(8,128)} %bitcast.66, bf16[2048,768]{1,0:T(8,128)(2,1)S(1)} %get-tuple-element.698, f32[2048]{0:T(1024)S(1)} %get-tuple-element.696, f32[512]{0:T(512)S(1)} %dynamic_slice.127, f32[512]{0:T(512)S(1)} %dynamic-slice_negate_fusion.4, s32[2048]{0:T(1024)S(1)} %fusion.77, ...), kind=kOutput, calls=%fused_computation.4.clone.1 | convolution fusion | flops 1619000832 | bytes 8151044 | tf_op jit(solution)/shard_map/while/body/eval_jaxpr/dot_general | solution.py:62
  205.5 5.7 %fusion.78 = f32[512]{0:T(512)S(1)} fusion(f32[64,8,16,128]{3,2,1,0:T(8,128)} %bitcast.66, bf16[2048,768]{1,0:T(8,128)(2,1)S(1)} %get-tuple-element.698, f32[2048]{0:T(1024)S(1)} %get-tuple-element.696, f32[512]{0:T(512)S(1)} %dynamic_slice.127, f32[512]{0:T(512)S(1)} %dynamic-slice_negate_fusion.4, s32[2048]{0:T(1024)S(1)} %fusion.77, ...), kind=kOutput, calls=%fused_computation.4.clone.1 | convolution fusion | flops 1619000832 | bytes 8151044 | tf_op jit(solution)/shard_map/while/body/eval_jaxpr/dot_general | solution.py:62
  218.3 5.7 %fusion.78 = f32[512]{0:T(512)S(1)} fusion(f32[64,8,16,128]{3,2,1,0:T(8,128)} %bitcast.66, bf16[2048,768]{1,0:T(8,128)(2,1)S(1)} %get-tuple-element.698, f32[2048]{0:T(1024)S(1)} %get-tuple-element.696, f32[512]{0:T(512)S(1)} %dynamic_slice.127, f32[512]{0:T(512)S(1)} %dynamic-slice_negate_fusion.4, s32[2048]{0:T(1024)S(1)} %fusion.77, ...), kind=kOutput, calls=%fused_computation.4.clone.1 | convolution fusion | flops 1619000832 | bytes 8151044 | tf_op jit(solution)/shard_map/while/body/eval_jaxpr/dot_general | solution.py:62
  224.0 51.3 %psum.14 = f32[4096]{0:T(1024)S(1)} all-reduce(f32[4096]{0:T(1024)S(1)} %bitcast.69), channel_id=1, replica_groups=mesh['row'=8,'col'=16] {'col'}, use_global_device_ids=true, to_apply=%region_5.6 | all-reduce | flops 4096 | bytes 32768 | tf_op jit(solution)/shard_map/psum | solution.py:81
  275.4 19.4 %all-gather.2 = f32[8,1,256]{2,1,0:T(1,128)S(1)} all-gather(f32[1,1,256]{2,1,0:T(1,128)S(1)} %bitcast.75), channel_id=1, replica_groups=mesh['row'=8,'col'=16] {'row'}, dimensions={0}, use_global_device_ids=true | all-gather | bytes 9216 | tf_op jit(solution)/shard_map/all_gather | solution.py:83
  294.8 114.9 %while.27 = (s32[]{:T(128)}, f32[8,512,256]{2,1,0:T(8,128)}, s32[8]{0:T(128)S(1)}, s32[4096]{0:T(1024)S(1)}, f32[32,16]{1,0:T(8,128)S(1)}, /*index=5*/f32[4096]{...) while((s32[]{:T(128)}, f32[8,512,256]{2,1,0:T(8,128)}, ...), condition=%wide.region_7.8_spmd.clone, body=%wide.region_6.7_spmd.clone.sunk | while | flops 2162196992 | bytes 13960894 | solution.py:96
  301.6 7.6 %fusion.83 = f32[8,512,256]{2,1,0:T(8,128)} fusion(f32[8,512,256]{2,1,0:T(8,128)} %get-tuple-element.730, s32[]{:T(128)} %get-tuple-element.729, bf16[2048,256]{1,0:T(8,128)(2,1)} %get-tuple-element.764, f32[64,8,16,128]{3,2,1,0:T(8,128)} %bitcast.65, bf16[2048,768]{1,0:T(8,128)(2,1)S(1)} %get-tuple-element.760, f32[2048]{0:T(1024)S(1)} %get-tuple-element.763, ...), kind=kOutput, calls=%fused_computation.28.clone.1 | convolution fusion | flops 2162163712 | bytes 9740804 | tf_op jit(solution)/shard_map/while/body/eval_jaxpr/dot_general | solution.py:93
  315.9 7.6 %fusion.83 = f32[8,512,256]{2,1,0:T(8,128)} fusion(f32[8,512,256]{2,1,0:T(8,128)} %get-tuple-element.730, s32[]{:T(128)} %get-tuple-element.729, bf16[2048,256]{1,0:T(8,128)(2,1)} %get-tuple-element.764, f32[64,8,16,128]{3,2,1,0:T(8,128)} %bitcast.65, bf16[2048,768]{1,0:T(8,128)(2,1)S(1)} %get-tuple-element.760, f32[2048]{0:T(1024)S(1)} %get-tuple-element.763, ...), kind=kOutput, calls=%fused_computation.28.clone.1 | convolution fusion | flops 2162163712 | bytes 9740804 | tf_op jit(solution)/shard_map/while/body/eval_jaxpr/dot_general | solution.py:93
  330.3 7.6 %fusion.83 = f32[8,512,256]{2,1,0:T(8,128)} fusion(f32[8,512,256]{2,1,0:T(8,128)} %get-tuple-element.730, s32[]{:T(128)} %get-tuple-element.729, bf16[2048,256]{1,0:T(8,128)(2,1)} %get-tuple-element.764, f32[64,8,16,128]{3,2,1,0:T(8,128)} %bitcast.65, bf16[2048,768]{1,0:T(8,128)(2,1)S(1)} %get-tuple-element.760, f32[2048]{0:T(1024)S(1)} %get-tuple-element.763, ...), kind=kOutput, calls=%fused_computation.28.clone.1 | convolution fusion | flops 2162163712 | bytes 9740804 | tf_op jit(solution)/shard_map/while/body/eval_jaxpr/dot_general | solution.py:93
  344.6 7.6 %fusion.83 = f32[8,512,256]{2,1,0:T(8,128)} fusion(f32[8,512,256]{2,1,0:T(8,128)} %get-tuple-element.730, s32[]{:T(128)} %get-tuple-element.729, bf16[2048,256]{1,0:T(8,128)(2,1)} %get-tuple-element.764, f32[64,8,16,128]{3,2,1,0:T(8,128)} %bitcast.65, bf16[2048,768]{1,0:T(8,128)(2,1)S(1)} %get-tuple-element.760, f32[2048]{0:T(1024)S(1)} %get-tuple-element.763, ...), kind=kOutput, calls=%fused_computation.28.clone.1 | convolution fusion | flops 2162163712 | bytes 9740804 | tf_op jit(solution)/shard_map/while/body/eval_jaxpr/dot_general | solution.py:93
  359.0 7.6 %fusion.83 = f32[8,512,256]{2,1,0:T(8,128)} fusion(f32[8,512,256]{2,1,0:T(8,128)} %get-tuple-element.730, s32[]{:T(128)} %get-tuple-element.729, bf16[2048,256]{1,0:T(8,128)(2,1)} %get-tuple-element.764, f32[64,8,16,128]{3,2,1,0:T(8,128)} %bitcast.65, bf16[2048,768]{1,0:T(8,128)(2,1)S(1)} %get-tuple-element.760, f32[2048]{0:T(1024)S(1)} %get-tuple-element.763, ...), kind=kOutput, calls=%fused_computation.28.clone.1 | convolution fusion | flops 2162163712 | bytes 9740804 | tf_op jit(solution)/shard_map/while/body/eval_jaxpr/dot_general | solution.py:93
  373.4 7.7 %fusion.83 = f32[8,512,256]{2,1,0:T(8,128)} fusion(f32[8,512,256]{2,1,0:T(8,128)} %get-tuple-element.730, s32[]{:T(128)} %get-tuple-element.729, bf16[2048,256]{1,0:T(8,128)(2,1)} %get-tuple-element.764, f32[64,8,16,128]{3,2,1,0:T(8,128)} %bitcast.65, bf16[2048,768]{1,0:T(8,128)(2,1)S(1)} %get-tuple-element.760, f32[2048]{0:T(1024)S(1)} %get-tuple-element.763, ...), kind=kOutput, calls=%fused_computation.28.clone.1 | convolution fusion | flops 2162163712 | bytes 9740804 | tf_op jit(solution)/shard_map/while/body/eval_jaxpr/dot_general | solution.py:93
  387.8 7.6 %fusion.83 = f32[8,512,256]{2,1,0:T(8,128)} fusion(f32[8,512,256]{2,1,0:T(8,128)} %get-tuple-element.730, s32[]{:T(128)} %get-tuple-element.729, bf16[2048,256]{1,0:T(8,128)(2,1)} %get-tuple-element.764, f32[64,8,16,128]{3,2,1,0:T(8,128)} %bitcast.65, bf16[2048,768]{1,0:T(8,128)(2,1)S(1)} %get-tuple-element.760, f32[2048]{0:T(1024)S(1)} %get-tuple-element.763, ...), kind=kOutput, calls=%fused_computation.28.clone.1 | convolution fusion | flops 2162163712 | bytes 9740804 | tf_op jit(solution)/shard_map/while/body/eval_jaxpr/dot_general | solution.py:93
  402.1 7.6 %fusion.83 = f32[8,512,256]{2,1,0:T(8,128)} fusion(f32[8,512,256]{2,1,0:T(8,128)} %get-tuple-element.730, s32[]{:T(128)} %get-tuple-element.729, bf16[2048,256]{1,0:T(8,128)(2,1)} %get-tuple-element.764, f32[64,8,16,128]{3,2,1,0:T(8,128)} %bitcast.65, bf16[2048,768]{1,0:T(8,128)(2,1)S(1)} %get-tuple-element.760, f32[2048]{0:T(1024)S(1)} %get-tuple-element.763, ...), kind=kOutput, calls=%fused_computation.28.clone.1 | convolution fusion | flops 2162163712 | bytes 9740804 | tf_op jit(solution)/shard_map/while/body/eval_jaxpr/dot_general | solution.py:93
  409.7 130.2 %all-reduce.2.cloned.1.call-done = f32[4096,256]{1,0:T(8,128)} async-done(((f32[4096,256]{1,0:T(8,128)}), f32[4096,256]{1,0:T(8,128)}) %all-reduce.2.cloned.1.call-update) | async-done | bytes 4194320 | tf_op jit(solution)/shard_map/psum | solution.py:97
  (153 shorter events, 48.5 us)
Async XLA Ops:
  6.5 68.8 %all-gather.9.cloned.1.call-start = ((), (), s32[]{:S(2)}) async-start(), calls=%async_computation.1 | async-start | bytes 3538944 | tf_op jit(solution)/shard_map/all_gather | solution.py:35
  7.3 110.6 %all-gather.7.cloned.1.call-start = ((), (), s32[]{:S(2)}) async-start(), calls=%async_computation | async-start | bytes 6684672 | tf_op jit(solution)/shard_map/all_gather | solution.py:31
  8.0 286.8 %all-gather.11.cloned.1.call-start = ((), (), s32[]{:S(2)}) async-start(), calls=%async_computation.2 | async-start | bytes 1179648 | tf_op jit(solution)/shard_map/all_gather | solution.py:37
  8.7 531.2 %all-reduce.2.cloned.1.call-start = ((), (), s32[]{:S(2)}) async-start(), calls=%async_computation.3 | async-start | bytes 8388608 | tf_op jit(solution)/shard_map/psum | solution.py:97
  75.3 46.6 %copy-start = (bf16[2048,768]{1,0:T(8,128)(2,1)S(1)}, bf16[2048,768]{1,0:T(8,128)(2,1)}, u32[]{:S(2)}) copy-start(bf16[2048,768]{1,0:T(8,128)(2,1)} %all-gather.9.cloned.1.call-done) | copy-start | bytes 9437188
Sparse Core Ops, SparseCore 0:
  9.7 65.6 all-gather.8
  77.0 40.7 all-gather.6
  120.2 45.7 all-gather.10
  409.9 130.0 all-reduce.1
where the time goes:
time: 549 us; the launch traced here: 548 us
  waiting for transfers between devices  193 us (35%)
  blocking collectives  112 us (20%)
  matrix products  109 us (20%)
  loops' own time  57.7 us (11%)
  local copies, waits for them, and re-layouts  54 us (10%)
  between operations  13.2 us (2%)
  other arithmetic  8.3 us (2%)
    psum x1, waiting for transfers between devices, shards(): summed = lax.psum(partial_out, 'col')  130 us
    dot_general x8, matrix products, one_block(): return jnp.dot(weight, cols_feat, preferred_element_type=jnp.float32)  61 us
    psum x1, blocking collectives, shards(): row_totals = lax.psum(row_partial, 'col')  51.3 us
    dot_general x8, matrix products, block_terms(): lax.dot_general(row_emb, cols_x, (((1,), (1,)), ((), ())), preferred_elem...  45.4 us
    all_gather x1, waiting for transfers between devices, shards(): lax.all_gather(embeddings, 'col', axis=0, tiled=True)  39.8 us
    broadcast_in_dim x16, local copies, waits for them, and re-layouts, block_terms(): jnp.broadcast_to(active_part[:, None, :, None], (size // BLK, BLK, col_bl...  38.6 us
    another operation x1, loops' own time, shards(): lax.map(lambda start: jnp.sum(block_terms(start, block_rows)[2], axis=1),...  30.1 us
    another operation x1, loops' own time, shards(): lax.map(one_block, begins).reshape(total_rows, cols_feat.shape[1])  27.6 us
  transfers between devices with their start and end apart: 4, of which 3 were waited for; matrix products, arithmetic and copies ran while one was open for 15% of the time, Pallas kernels for 0%

commit v1 on v0

--- a/solution.py
+++ b/solution.py
@@ -78,7 +78,8 @@
     row_partial = lax.map(
         lambda start: jnp.sum(block_terms(start, block_rows)[2], axis=1), starts
     ).reshape(total_rows)
-    row_totals = lax.psum(row_partial, "col")
+    pieces = lax.all_gather(row_partial, "col", axis=0, tiled=False)
+    row_totals = pieces.sum(axis=0)
     own_totals = lax.dynamic_slice_in_dim(row_totals, col_index * own_count, own_count, 0)
     col_totals = lax.all_gather(own_totals, "row", axis=0, tiled=True)
     size = math.gcd(total_rows, 512)

time: 549 us -> 513 us (0.934)
  blocking collectives: 112 us -> 80.8 us
    psum x1 -> x0, blocking collectives: 51.3 us -> none  [shards(): row_totals = lax.psum(row_partial, 'col')]
    all_gather x0 -> x1, blocking collectives: none -> 19.6 us  [shards(): pieces = lax.all_gather(row_partial, 'col', axis=0, tiled=False)]
  transfers between devices with their start and end apart: 4 -> 4, of which waited for: 3 -> 3; matrix products, arithmetic and copies ran while one was open for 15% -> 16% of each run, Pallas kernels for 0% -> 0%
where the time goes in v1:
time: 513 us; the launch traced here: 512 us
  waiting for transfers between devices  189 us (37%)
  matrix products  109 us (21%)
  blocking collectives  80.8 us (16%)
  loops' own time  57.7 us (11%)
  local copies, waits for them, and re-layouts  54.1 us (11%)
  between operations  13.2 us (3%)
  other arithmetic  8.47 us (2%)
    psum x1, waiting for transfers between devices, shards(): summed = lax.psum(partial_out, 'col')  126 us
    dot_general x8, matrix products, one_block(): return jnp.dot(weight, cols_feat, preferred_element_type=jnp.float32)  60.9 us
    dot_general x8, matrix products, block_terms(): lax.dot_general(row_emb, cols_x, (((1,), (1,)), ((), ())), preferred_elem...  45.2 us
    all_gather x1, waiting for transfers between devices, shards(): lax.all_gather(embeddings, 'col', axis=0, tiled=True)  39.8 us
    broadcast_in_dim x16, local copies, waits for them, and re-layouts, block_terms(): jnp.broadcast_to(active_part[:, None, :, None], (size // BLK, BLK, col_bl...  38.6 us
    another operation x1, loops' own time, shards(): lax.map(lambda start: jnp.sum(block_terms(start, block_rows)[2], axis=1),...  30.1 us
    another operation x1, loops' own time, shards(): lax.map(one_block, begins).reshape(total_rows, cols_feat.shape[1])  27.6 us
    all_gather x1, blocking collectives, shards(): lax.all_gather(spread, 'col', axis=0, tiled=True)  21.2 us
  transfers between devices with their start and end apart: 4, of which 3 were waited for; matrix products, arithmetic and copies ran while one was open for 16% of the time, Pallas kernels for 0%

profile of v1, /device:TPU:1, one launch (start us, length us, event | category | flops | bytes accessed | tf_op | source)
XLA Modules:
  0.0 512.2 jit_solution(4506874127202068376)
XLA Ops:
  9.5 21.2 %all-gather = bf16[16,1,256]{2,1,0:T(2,128)(2,1)S(1)} all-gather(bf16[1,1,256]{2,1,0:T(2,128)(2,1)S(1)} %reshape.40), channel_id=1, replica_groups=mesh['row'=8,'col'=16] {'col'}, dimensions={0}, use_global_device_ids=true | all-gather | bytes 8704 | tf_op jit(solution)/shard_map/all_gather | solution.py:32
  30.6 20.6 %all-gather.2 = bf16[8,1,256]{2,1,0:T(2,128)(2,1)S(1)} all-gather(bf16[1,1,256]{2,1,0:T(2,128)(2,1)S(1)} %reshape.40), channel_id=1, replica_groups=mesh['row'=8,'col'=16] {'row'}, dimensions={0}, use_global_device_ids=true | all-gather | bytes 4608 | tf_op jit(solution)/shard_map/all_gather | solution.py:36
  54.4 21.0 %all-gather.10.cloned.1.call-done = bf16[2048,768]{1,0:T(8,128)(2,1)} async-done(((bf16[256,768]{1,0:T(8,128)(2,1)}), bf16[2048,768]{1,0:T(8,128)(2,1)}) %all-gather.10.cloned.1.call-update) | async-done | bytes 3145744 | tf_op jit(solution)/shard_map/all_gather | solution.py:35
  75.3 2.7 multiply_reduce_fusion.1
  78.1 39.8 %all-gather.8.cloned.1.call-done = bf16[4096,768]{1,0:T(8,128)(2,1)} async-done(((bf16[256,768]{1,0:T(8,128)(2,1)}), bf16[4096,768]{1,0:T(8,128)(2,1)}) %all-gather.8.cloned.1.call-update) | async-done | bytes 6291472 | tf_op jit(solution)/shard_map/all_gather | solution.py:31
  117.9 4.1 multiply_reduce_fusion
  122.0 101.8 %while.26 = (s32[]{:T(128)}, f32[8,512]{1,0:T(8,128)S(1)}, s32[8]{0:T(128)S(1)}, s32[4096]{0:T(1024)S(1)}, f32[32,16]{1,0:T(8,128)S(1)}, /*index=5*/f32[4096]{0:...) while((s32[]{:T(128)}, f32[8,512]{1,0:T(8,128)S(1)}, ...), condition=%wide.region_4.5_spmd.clone, body=%wide.region_2.4_spmd.clone.sunk | while | flops 1619034112 | bytes 12371102 | solution.py:78
  125.1 2.4 broadcast_in_dim.65
  129.0 5.7 %fusion.78 = f32[512]{0:T(512)S(1)} fusion(f32[64,8,16,128]{3,2,1,0:T(8,128)} %bitcast.64, bf16[2048,768]{1,0:T(8,128)(2,1)S(1)} %get-tuple-element.698, f32[2048]{0:T(1024)S(1)} %get-tuple-element.696, f32[512]{0:T(512)S(1)} %dynamic_slice.127, f32[512]{0:T(512)S(1)} %dynamic-slice_negate_fusion.4, s32[2048]{0:T(1024)S(1)} %fusion.77, ...), kind=kOutput, calls=%fused_computation.4.clone.1 | convolution fusion | flops 1619000832 | bytes 8151044 | tf_op jit(solution)/shard_map/while/body/eval_jaxpr/dot_general | solution.py:62
  137.9 2.4 broadcast_in_dim.65
  141.8 5.6 %fusion.78 = f32[512]{0:T(512)S(1)} fusion(f32[64,8,16,128]{3,2,1,0:T(8,128)} %bitcast.64, bf16[2048,768]{1,0:T(8,128)(2,1)S(1)} %get-tuple-element.698, f32[2048]{0:T(1024)S(1)} %get-tuple-element.696, f32[512]{0:T(512)S(1)} %dynamic_slice.127, f32[512]{0:T(512)S(1)} %dynamic-slice_negate_fusion.4, s32[2048]{0:T(1024)S(1)} %fusion.77, ...), kind=kOutput, calls=%fused_computation.4.clone.1 | convolution fusion | flops 1619000832 | bytes 8151044 | tf_op jit(solution)/shard_map/while/body/eval_jaxpr/dot_general | solution.py:62
  150.6 2.4 broadcast_in_dim.65
  154.5 5.6 %fusion.78 = f32[512]{0:T(512)S(1)} fusion(f32[64,8,16,128]{3,2,1,0:T(8,128)} %bitcast.64, bf16[2048,768]{1,0:T(8,128)(2,1)S(1)} %get-tuple-element.698, f32[2048]{0:T(1024)S(1)} %get-tuple-element.696, f32[512]{0:T(512)S(1)} %dynamic_slice.127, f32[512]{0:T(512)S(1)} %dynamic-slice_negate_fusion.4, s32[2048]{0:T(1024)S(1)} %fusion.77, ...), kind=kOutput, calls=%fused_computation.4.clone.1 | convolution fusion | flops 1619000832 | bytes 8151044 | tf_op jit(solution)/shard_map/while/body/eval_jaxpr/dot_general | solution.py:62
  163.3 2.4 broadcast_in_dim.65
  167.2 5.6 %fusion.78 = f32[512]{0:T(512)S(1)} fusion(f32[64,8,16,128]{3,2,1,0:T(8,128)} %bitcast.64, bf16[2048,768]{1,0:T(8,128)(2,1)S(1)} %get-tuple-element.698, f32[2048]{0:T(1024)S(1)} %get-tuple-element.696, f32[512]{0:T(512)S(1)} %dynamic_slice.127, f32[512]{0:T(512)S(1)} %dynamic-slice_negate_fusion.4, s32[2048]{0:T(1024)S(1)} %fusion.77, ...), kind=kOutput, calls=%fused_computation.4.clone.1 | convolution fusion | flops 1619000832 | bytes 8151044 | tf_op jit(solution)/shard_map/while/body/eval_jaxpr/dot_general | solution.py:62
  176.1 2.4 broadcast_in_dim.65
  180.0 5.6 %fusion.78 = f32[512]{0:T(512)S(1)} fusion(f32[64,8,16,128]{3,2,1,0:T(8,128)} %bitcast.64, bf16[2048,768]{1,0:T(8,128)(2,1)S(1)} %get-tuple-element.698, f32[2048]{0:T(1024)S(1)} %get-tuple-element.696, f32[512]{0:T(512)S(1)} %dynamic_slice.127, f32[512]{0:T(512)S(1)} %dynamic-slice_negate_fusion.4, s32[2048]{0:T(1024)S(1)} %fusion.77, ...), kind=kOutput, calls=%fused_computation.4.clone.1 | convolution fusion | flops 1619000832 | bytes 8151044 | tf_op jit(solution)/shard_map/while/body/eval_jaxpr/dot_general | solution.py:62
  192.7 5.6 %fusion.78 = f32[512]{0:T(512)S(1)} fusion(f32[64,8,16,128]{3,2,1,0:T(8,128)} %bitcast.64, bf16[2048,768]{1,0:T(8,128)(2,1)S(1)} %get-tuple-element.698, f32[2048]{0:T(1024)S(1)} %get-tuple-element.696, f32[512]{0:T(512)S(1)} %dynamic_slice.127, f32[512]{0:T(512)S(1)} %dynamic-slice_negate_fusion.4, s32[2048]{0:T(1024)S(1)} %fusion.77, ...), kind=kOutput, calls=%fused_computation.4.clone.1 | convolution fusion | flops 1619000832 | bytes 8151044 | tf_op jit(solution)/shard_map/while/body/eval_jaxpr/dot_general | solution.py:62
  205.4 5.6 %fusion.78 = f32[512]{0:T(512)S(1)} fusion(f32[64,8,16,128]{3,2,1,0:T(8,128)} %bitcast.64, bf16[2048,768]{1,0:T(8,128)(2,1)S(1)} %get-tuple-element.698, f32[2048]{0:T(1024)S(1)} %get-tuple-element.696, f32[512]{0:T(512)S(1)} %dynamic_slice.127, f32[512]{0:T(512)S(1)} %dynamic-slice_negate_fusion.4, s32[2048]{0:T(1024)S(1)} %fusion.77, ...), kind=kOutput, calls=%fused_computation.4.clone.1 | convolution fusion | flops 1619000832 | bytes 8151044 | tf_op jit(solution)/shard_map/while/body/eval_jaxpr/dot_general | solution.py:62
  218.1 5.6 %fusion.78 = f32[512]{0:T(512)S(1)} fusion(f32[64,8,16,128]{3,2,1,0:T(8,128)} %bitcast.64, bf16[2048,768]{1,0:T(8,128)(2,1)S(1)} %get-tuple-element.698, f32[2048]{0:T(1024)S(1)} %get-tuple-element.696, f32[512]{0:T(512)S(1)} %dynamic_slice.127, f32[512]{0:T(512)S(1)} %dynamic-slice_negate_fusion.4, s32[2048]{0:T(1024)S(1)} %fusion.77, ...), kind=kOutput, calls=%fused_computation.4.clone.1 | convolution fusion | flops 1619000832 | bytes 8151044 | tf_op jit(solution)/shard_map/while/body/eval_jaxpr/dot_general | solution.py:62
  223.8 19.6 %all-gather.1 = f32[16,1,4096]{2,1,0:T(1,128)S(1)} all-gather(f32[1,1,4096]{2,1,0:T(1,128)S(1)} %reshape.42), channel_id=1, replica_groups=mesh['row'=8,'col'=16] {'col'}, dimensions={0}, use_global_device_ids=true | all-gather | bytes 278528 | tf_op jit(solution)/shard_map/all_gather | solution.py:81
  243.7 19.4 %all-gather.3 = f32[8,1,256]{2,1,0:T(1,128)S(1)} all-gather(f32[1,1,256]{2,1,0:T(1,128)S(1)} %bitcast.71), channel_id=1, replica_groups=mesh['row'=8,'col'=16] {'row'}, dimensions={0}, use_global_device_ids=true | all-gather | bytes 9216 | tf_op jit(solution)/shard_map/all_gather | solution.py:84
  263.1 114.8 %while.27 = (s32[]{:T(128)}, f32[8,512,256]{2,1,0:T(8,128)}, s32[8]{0:T(128)S(1)}, s32[4096]{0:T(1024)S(1)}, f32[32,16]{1,0:T(8,128)S(1)}, /*index=5*/f32[4096]{...) while((s32[]{:T(128)}, f32[8,512,256]{2,1,0:T(8,128)}, ...), condition=%wide.region_7.8_spmd.clone, body=%wide.region_6.7_spmd.clone.sunk | while | flops 2162196992 | bytes 13960894 | solution.py:97
  269.9 7.6 %fusion.83 = f32[8,512,256]{2,1,0:T(8,128)} fusion(f32[8,512,256]{2,1,0:T(8,128)} %get-tuple-element.730, s32[]{:T(128)} %get-tuple-element.729, bf16[2048,256]{1,0:T(8,128)(2,1)} %get-tuple-element.764, f32[64,8,16,128]{3,2,1,0:T(8,128)} %bitcast.63, bf16[2048,768]{1,0:T(8,128)(2,1)S(1)} %get-tuple-element.760, f32[2048]{0:T(1024)S(1)} %get-tuple-element.763, ...), kind=kOutput, calls=%fused_computation.28.clone.1 | convolution fusion | flops 2162163712 | bytes 9740804 | tf_op jit(solution)/shard_map/while/body/eval_jaxpr/dot_general | solution.py:94
  284.2 7.6 %fusion.83 = f32[8,512,256]{2,1,0:T(8,128)} fusion(f32[8,512,256]{2,1,0:T(8,128)} %get-tuple-element.730, s32[]{:T(128)} %get-tuple-element.729, bf16[2048,256]{1,0:T(8,128)(2,1)} %get-tuple-element.764, f32[64,8,16,128]{3,2,1,0:T(8,128)} %bitcast.63, bf16[2048,768]{1,0:T(8,128)(2,1)S(1)} %get-tuple-element.760, f32[2048]{0:T(1024)S(1)} %get-tuple-element.763, ...), kind=kOutput, calls=%fused_computation.28.clone.1 | convolution fusion | flops 2162163712 | bytes 9740804 | tf_op jit(solution)/shard_map/while/body/eval_jaxpr/dot_general | solution.py:94
  298.6 7.6 %fusion.83 = f32[8,512,256]{2,1,0:T(8,128)} fusion(f32[8,512,256]{2,1,0:T(8,128)} %get-tuple-element.730, s32[]{:T(128)} %get-tuple-element.729, bf16[2048,256]{1,0:T(8,128)(2,1)} %get-tuple-element.764, f32[64,8,16,128]{3,2,1,0:T(8,128)} %bitcast.63, bf16[2048,768]{1,0:T(8,128)(2,1)S(1)} %get-tuple-element.760, f32[2048]{0:T(1024)S(1)} %get-tuple-element.763, ...), kind=kOutput, calls=%fused_computation.28.clone.1 | convolution fusion | flops 2162163712 | bytes 9740804 | tf_op jit(solution)/shard_map/while/body/eval_jaxpr/dot_general | solution.py:94
  312.9 7.6 %fusion.83 = f32[8,512,256]{2,1,0:T(8,128)} fusion(f32[8,512,256]{2,1,0:T(8,128)} %get-tuple-element.730, s32[]{:T(128)} %get-tuple-element.729, bf16[2048,256]{1,0:T(8,128)(2,1)} %get-tuple-element.764, f32[64,8,16,128]{3,2,1,0:T(8,128)} %bitcast.63, bf16[2048,768]{1,0:T(8,128)(2,1)S(1)} %get-tuple-element.760, f32[2048]{0:T(1024)S(1)} %get-tuple-element.763, ...), kind=kOutput, calls=%fused_computation.28.clone.1 | convolution fusion | flops 2162163712 | bytes 9740804 | tf_op jit(solution)/shard_map/while/body/eval_jaxpr/dot_general | solution.py:94
  327.2 7.6 %fusion.83 = f32[8,512,256]{2,1,0:T(8,128)} fusion(f32[8,512,256]{2,1,0:T(8,128)} %get-tuple-element.730, s32[]{:T(128)} %get-tuple-element.729, bf16[2048,256]{1,0:T(8,128)(2,1)} %get-tuple-element.764, f32[64,8,16,128]{3,2,1,0:T(8,128)} %bitcast.63, bf16[2048,768]{1,0:T(8,128)(2,1)S(1)} %get-tuple-element.760, f32[2048]{0:T(1024)S(1)} %get-tuple-element.763, ...), kind=kOutput, calls=%fused_computation.28.clone.1 | convolution fusion | flops 2162163712 | bytes 9740804 | tf_op jit(solution)/shard_map/while/body/eval_jaxpr/dot_general | solution.py:94
  341.6 7.7 %fusion.83 = f32[8,512,256]{2,1,0:T(8,128)} fusion(f32[8,512,256]{2,1,0:T(8,128)} %get-tuple-element.730, s32[]{:T(128)} %get-tuple-element.729, bf16[2048,256]{1,0:T(8,128)(2,1)} %get-tuple-element.764, f32[64,8,16,128]{3,2,1,0:T(8,128)} %bitcast.63, bf16[2048,768]{1,0:T(8,128)(2,1)S(1)} %get-tuple-element.760, f32[2048]{0:T(1024)S(1)} %get-tuple-element.763, ...), kind=kOutput, calls=%fused_computation.28.clone.1 | convolution fusion | flops 2162163712 | bytes 9740804 | tf_op jit(solution)/shard_map/while/body/eval_jaxpr/dot_general | solution.py:94
  356.0 7.6 %fusion.83 = f32[8,512,256]{2,1,0:T(8,128)} fusion(f32[8,512,256]{2,1,0:T(8,128)} %get-tuple-element.730, s32[]{:T(128)} %get-tuple-element.729, bf16[2048,256]{1,0:T(8,128)(2,1)} %get-tuple-element.764, f32[64,8,16,128]{3,2,1,0:T(8,128)} %bitcast.63, bf16[2048,768]{1,0:T(8,128)(2,1)S(1)} %get-tuple-element.760, f32[2048]{0:T(1024)S(1)} %get-tuple-element.763, ...), kind=kOutput, calls=%fused_computation.28.clone.1 | convolution fusion | flops 2162163712 | bytes 9740804 | tf_op jit(solution)/shard_map/while/body/eval_jaxpr/dot_general | solution.py:94
  370.4 7.6 %fusion.83 = f32[8,512,256]{2,1,0:T(8,128)} fusion(f32[8,512,256]{2,1,0:T(8,128)} %get-tuple-element.730, s32[]{:T(128)} %get-tuple-element.729, bf16[2048,256]{1,0:T(8,128)(2,1)} %get-tuple-element.764, f32[64,8,16,128]{3,2,1,0:T(8,128)} %bitcast.63, bf16[2048,768]{1,0:T(8,128)(2,1)S(1)} %get-tuple-element.760, f32[2048]{0:T(1024)S(1)} %get-tuple-element.763, ...), kind=kOutput, calls=%fused_computation.28.clone.1 | convolution fusion | flops 2162163712 | bytes 9740804 | tf_op jit(solution)/shard_map/while/body/eval_jaxpr/dot_general | solution.py:94
  378.0 126.0 %all-reduce.2.cloned.1.call-done = f32[4096,256]{1,0:T(8,128)} async-done(((f32[4096,256]{1,0:T(8,128)}), f32[4096,256]{1,0:T(8,128)}) %all-reduce.2.cloned.1.call-update) | async-done | bytes 4194320 | tf_op jit(solution)/shard_map/psum | solution.py:98
  (154 shorter events, 48.8 us)
Async XLA Ops:
  6.5 68.8 %all-gather.10.cloned.1.call-start = ((), (), s32[]{:S(2)}) async-start(), calls=%async_computation.1 | async-start | bytes 3538944 | tf_op jit(solution)/shard_map/all_gather | solution.py:35
  7.3 110.6 %all-gather.8.cloned.1.call-start = ((), (), s32[]{:S(2)}) async-start(), calls=%async_computation | async-start | bytes 6684672 | tf_op jit(solution)/shard_map/all_gather | solution.py:31
  8.0 255.1 %all-gather.12.cloned.1.call-start = ((), (), s32[]{:S(2)}) async-start(), calls=%async_computation.2 | async-start | bytes 1179648 | tf_op jit(solution)/shard_map/all_gather | solution.py:37
  8.7 495.2 %all-reduce.2.cloned.1.call-start = ((), (), s32[]{:S(2)}) async-start(), calls=%async_computation.3 | async-start | bytes 8388608 | tf_op jit(solution)/shard_map/psum | solution.py:98
  75.3 46.6 %copy-start = (bf16[2048,768]{1,0:T(8,128)(2,1)S(1)}, bf16[2048,768]{1,0:T(8,128)(2,1)}, u32[]{:S(2)}) copy-start(bf16[2048,768]{1,0:T(8,128)(2,1)} %all-gather.10.cloned.1.call-done) | copy-start | bytes 9437188
Sparse Core Ops, SparseCore 0:
  9.7 65.6 all-gather.9
  77.0 40.7 all-gather.7
  120.2 45.7 all-gather.11
  378.1 125.8 all-reduce.1
